TPU v7x, 32 devices: a whole 2x2x4 slice. The times are simulated.
32 devices in a mesh: grp: 4 (over z), dev: 8 (over y, x, core).
Axes of the slice: x: 2, y: 2, z: 4, core: 2. Of those that a mesh axis runs over, the one named last changes fastest.
Arguments:
- fraction: float32 [64, 256, 1024], P('grp', 'dev'), may hold values from 0 to 1
- courant: float32 [64, 256, 1024], P('grp', 'dev'), may hold values from -0.45 to 0.45
- divergence: float32 [64, 256, 1024], P('grp', 'dev'), may hold values from -40 to 40
- densities: float32 [2], replicated, may hold values from 0.8 to 2.2
- band_tiles: int32 [4, 8, 128], P('grp', 'dev'), may hold values from -1 to 127, as said below
Outputs:
- new_fraction: float32 [64, 256, 1024], P('grp', 'dev')
- pressure: float32 [64, 256, 1024], P('grp', 'dev')
- residual: float32 [64, 256, 1024], P('grp', 'dev')
Inputs may be any that keep to these rules, and one draw needn't show every extreme that they name: `band_tiles`: each list holds distinct tile numbers first and -1 after them. In every group along dev the lists name 32 tiles a device on average, exactly, and one device of every group lists all 128 of its tiles.
All inputs are finite; a program needn't handle non-finite values.
Results may differ from a plain program's by a relative error of at most 0.012.
Values sent between devices are 32-bit elements; how exact they have to be, the bound alone decides.
A program may use at most 192 MiB of HBM per device.

v0:
```python
import jax
import jax.numpy as jnp
from jax import lax
from jax.sharding import PartitionSpec as P

TILE = 16
ITERS = 2


def with_halo(value, sides, width):
    for axis, dim in sides:
        size, length = (lax.axis_size(axis), value.shape[dim])
        up = [(i, (i + 1) % size) for i in range(size - 1)]
        down = [(j, i) for i, j in up]
        last = lax.slice_in_dim(value, length - width, length, axis=dim)
        first = lax.slice_in_dim(value, 0, width, axis=dim)
        before = lax.ppermute(last, axis, up)
        after = lax.ppermute(first, axis, down)
        value = jnp.concatenate([before, value, after], axis=dim)
    return value


def advect(extended, speeds):
    forward = extended[..., 1:] - extended[..., :-1]
    ahead_diff = forward[..., 1:]
    behind = forward[..., :-1]
    slopes = (
        0.5
        * (jnp.sign(ahead_diff) + jnp.sign(behind))
        * jnp.minimum(jnp.abs(ahead_diff), jnp.abs(behind))
    )
    face_span = speeds.shape[-1] - 1
    left_cell = extended[..., 1 : face_span + 2]
    right_cell = extended[..., 2 : face_span + 3]
    slope_left = slopes[..., 0 : face_span + 1]
    slope_right = slopes[..., 1 : face_span + 2]
    fluxes = jnp.where(
        speeds > 0,
        speeds * (left_cell + 0.5 * (1.0 - speeds) * slope_left),
        speeds * (right_cell - 0.5 * (1.0 + speeds) * slope_right),
    )
    return jnp.clip(
        extended[..., 2 : face_span + 2] - (fluxes[..., 1:] - fluxes[..., :-1]), 0.0, 1.0
    )


def coefficients(density):
    beta_first = 2.0 / (density[:-1, 1:-1, 1:-1] + density[1:, 1:-1, 1:-1])
    beta_second = 2.0 / (density[1:-1, :-1, 1:-1] + density[1:-1, 1:, 1:-1])
    beta_third = 2.0 / (density[1:-1, 1:-1, :-1] + density[1:-1, 1:-1, 1:])
    return (beta_first, beta_second, beta_third)


def apply_operator(field, padded, betas):
    beta_first, beta_second, beta_third = betas
    result = beta_first[1:] * (field - padded[2:, 1:-1, 1:-1]) + beta_first[:-1] * (
        field - padded[:-2, 1:-1, 1:-1]
    )
    result = (
        result
        + beta_second[:, 1:] * (field - padded[1:-1, 2:, 1:-1])
        + beta_second[:, :-1] * (field - padded[1:-1, :-2, 1:-1])
    )
    result = (
        result
        + beta_third[:, :, 1:] * (field - padded[1:-1, 1:-1, 2:])
        + beta_third[:, :, :-1] * (field - padded[1:-1, 1:-1, :-2])
    )
    return result


def operate_padded(field, rimmed, betas):
    padded = jnp.pad(rimmed, ((0, 0), (0, 0), (1, 1)))
    return apply_operator(field, padded, betas)


def operate(field, betas):
    rimmed = with_halo(field, (("grp", 0), ("dev", 1)), 1)
    return operate_padded(field, rimmed, betas)


def squares(residual):
    return lax.psum(jnp.sum(residual * residual), ("grp", "dev"))


def on_device(fraction, courant, divergence, densities, band_tiles):
    block_shape = fraction.shape
    depth_cells = block_shape[0]
    second_cells = block_shape[1]
    third_cells = block_shape[2]
    across = second_cells // TILE
    along_y = third_cells // TILE
    tile_total = across * along_y
    y_index = lax.broadcasted_iota(jnp.int32, block_shape, 2)
    speed_field = jnp.where(y_index > 0, courant, jnp.zeros_like(courant))
    band_list = band_tiles.reshape(tile_total)
    tile_ids = jnp.arange(tile_total, dtype=jnp.int32)
    extended = jnp.pad(fraction, ((0, 0), (0, 0), (2, 2)))
    speeds = jnp.concatenate(
        [speed_field, jnp.zeros((depth_cells, second_cells, 1), jnp.float32)], axis=2
    )
    advected = advect(extended, speeds)
    present = jnp.any(band_list[:, None] == tile_ids[None, :], axis=0)
    in_band = jnp.broadcast_to(
        present.reshape(1, across, 1, along_y, 1), (TILE, across, TILE, along_y, TILE)
    ).reshape(block_shape)
    new_fraction = jnp.where(in_band, advected, fraction)
    outer = with_halo(fraction, (("grp", 0), ("dev", 1)), 1)
    outer = jnp.pad(outer, ((0, 0), (0, 0), (1, 1)))
    density = outer * densities[0] + (1.0 - outer) * densities[1]
    betas = coefficients(density)
    first_image = operate(divergence, betas)
    pressure = jnp.zeros_like(divergence)
    residual = divergence
    direction = divergence
    norm_now = squares(residual)
    for iteration in range(ITERS):
        if iteration == 0:
            image_vec = first_image
        else:
            image_vec = operate(direction, betas)
        step_length = norm_now / lax.psum(jnp.sum(direction * image_vec), ("grp", "dev"))
        pressure = pressure + step_length * direction
        residual = residual - step_length * image_vec
        norm_next = squares(residual)
        direction = residual + norm_next / norm_now * direction
        norm_now = norm_next
    return (new_fraction, pressure, residual)


def solution(mesh):
    placed = (
        P("grp", "dev", None),
        P("grp", "dev", None),
        P("grp", "dev", None),
        P(),
        P("grp", "dev", None),
    )
    return jax.shard_map(
        on_device,
        mesh=mesh,
        in_specs=placed,
        out_specs=(P("grp", "dev", None), P("grp", "dev", None), P("grp", "dev", None)),
        check_vma=False,
    )
```

profile of v0, /device:TPU:0, one launch (start us, length us, event | category | flops | bytes accessed | tf_op | source)
XLA Modules:
  0.0 233.2 jit_solution(4330479886519162161)
XLA Ops:
  0.6 1.1 fusion.47
  1.8 1.3 collective-permute-start.4
  3.1 5.6 %collective-permute-start.5 = (f32[1,32,1024]{2,1,0:T(8,128)S(1)}, f32[1,32,1024]{2,1,0:T(8,128)S(1)}, u32[]{:S(2)}, u32[]{:S(2)}) collective-permute-start(f32[1,32,1024]{2,1,0:T(8,128)S(1)} %get-tuple-element.30), channel_id=1, source_target_pairs={{0,8},{8,16},{16,24},{1,9},{9,17},{17,25},{2,10},{10,18},{18,26},{... | collective-permute-start | bytes 393224 | tf_op jit(solution)/shard_map/ppermute | solution.py:17
  8.7 1.0 fusion.46
  9.7 3.9 %collective-permute-start = (f32[1,32,1024]{2,1,0:T(8,128)S(1)}, f32[1,32,1024]{2,1,0:T(8,128)S(1)}, u32[]{:S(2)}, u32[]{:S(2)}) collective-permute-start(f32[1,32,1024]{2,1,0:T(8,128)S(1)} %get-tuple-element.28), channel_id=1, source_target_pairs={{0,8},{8,16},{16,24},{1,9},{9,17},{17,25},{2,10},{10,18},{18,26},{... | collective-permute-start | bytes 393224 | tf_op jit(solution)/shard_map/ppermute | solution.py:17
  13.6 1.3 collective-permute-start.1
  14.9 2.7 %multiply_reduce_fusion.3 = f32[]{:T(128)} fusion(f32[16,32,1024]{2,1,0:T(8,128)} %param.7), kind=kLoop, calls=%fused_computation.92 | loop fusion | flops 1048575 | bytes 2097156 | tf_op jit(solution)/shard_map/reduce_sum | solution.py:83
  17.6 1.3 slice_subtract_fusion
  19.0 3.0 %minimum_multiply_fusion = f32[16,32,1026]{2,1,0:T(8,128)} fusion(f32[16,32,1027]{2,1,0:T(8,128)S(1)} %slice_subtract_fusion), kind=kLoop, calls=%fused_computation.27 | loop fusion | flops 4202496 | bytes 6303744 | tf_op jit(solution)/shard_map/mul | solution.py:28
  22.0 0.6 fusion.48
  22.6 1.2 copy.72
  23.8 1.2 copy.57
  25.0 0.1 copy.56
  25.2 0.1 copy.58
  25.3 1.3 collective-permute-start.2
  26.6 1.3 collective-permute-start.3
  28.0 0.1 copy.60
  28.3 1.3 collective-permute-start.6
  29.6 5.6 %collective-permute-start.7 = (f32[18,1,1024]{2,0,1:T(8,128)S(1)}, f32[18,1,1024]{2,0,1:T(8,128)S(1)}, u32[]{:S(2)}, u32[]{:S(2)}) collective-permute-start(f32[18,1,1024]{2,0,1:T(8,128)S(1)} %get-tuple-element.22), channel_id=1, source_target_pairs={{0,1},{1,2},{2,3},{3,4},{4,5},{5,6},{6,7},{8,9},{9,10},{10,11},{11... | collective-permute-start | bytes 221192 | tf_op jit(solution)/shard_map/ppermute | solution.py:17
  35.2 4.9 %multiply_add_fusion = f32[18,34,1026]{2,0,1:T(8,128)S(1)} fusion(f32[18,1,1024]{2,0,1:T(8,128)S(1)} %collective-permute-done.3, f32[1,32,1024]{2,0,1:T(1,128)S(1)} %copy.58, f32[16,32,1024]{2,0,1:T(8,128)S(1)} %copy.57, f32[1,32,1024]{2,0,1:T(1,128)S(1)} %copy.56, f32[18,1,1024]{2,0,1:T(8,128)S(1)} %collective-permute-done.2, f32[]{:T(128)} %bitcast.2, ...), kind=kLoop, calls=%fused_computation.14 | loop fusion | flops 10046592 | bytes 5018408 | tf_op jit(solution)/shard_map/add | solution.py:110
  40.1 1.9 fusion.1
  42.1 0.9 fusion.2
  43.0 1.2 fusion.8
  44.2 3.7 %select_maximum_fusion.4 = f32[18,34,1026]{2,0,1:T(8,128)S(1)} fusion(f32[18,1,1024]{2,0,1:T(8,128)S(1)} %collective-permute-done.6, f32[18,1,1024]{2,0,1:T(8,128)S(1)} %collective-permute-done.7, f32[1,32,1024]{2,0,1:T(1,128)S(1)} %copy.60, f32[16,32,1024]{2,0,1:T(8,128)S(1)} %copy.72, f32[1,32,1024]{2,0,1:T(1,128)S(1)} %copy.62), kind=kLoop, calls=%fused_computation.6 | loop fusion | flops 7534944 | bytes 5018400 | tf_op jit(solution)/shard_map/concatenate | solution.py:19
  47.9 8.1 %multiply_reduce_fusion.2 = (f32[]{:T(128)}, f32[16,32,1024]{2,0,1:T(8,128)}) fusion(f32[16,32,1024]{2,1,0:T(8,128)S(1)} %copy-done, f32[16,32,1024]{2,0,1:T(8,128)S(1)} %copy.72, f32[18,34,1026]{2,0,1:T(8,128)S(1)} %select_maximum_fusion.4, f32[16,32,1025]{2,0,1:T(8,128)S(1)} %fusion.2, f32[1,32,1024]{2,0,1:T(1,128)S(1)} %copy.60, ...), kind=kLoop, calls=%fused_computation.91 | loop fusion | flops 14155775 | bytes 23478276 | tf_op jit(solution)/shard_map/reduce_sum | solution.py:122
  56.0 43.1 %all-reduce.5 = (f32[]{:T(128)}, f32[]{:T(128)}) all-reduce(f32[]{:T(128)} %multiply_reduce_fusion.3, f32[]{:T(128)} %get-tuple-element.16), channel_id=1, replica_groups=mesh['grp'=4,'dev'=8] {'grp','dev'}, use_global_device_ids=true, to_apply=%region_2.3 | all-reduce | flops 2 | bytes 16 | tf_op jit(solution)/shard_map/psum | solution.py:83
  100.4 3.5 %multiply_reduce_fusion.1 = f32[]{:T(128)} fusion(f32[16,32,1024]{2,0,1:T(8,128)} %get-tuple-element.17, f32[]{:T(128)S(6)} %div.33, f32[16,32,1024]{2,1,0:T(8,128)S(1)} %copy-done), kind=kLoop, calls=%fused_computation.89 | loop fusion | flops 2097151 | bytes 4194312 | tf_op jit(solution)/shard_map/reduce_sum | solution.py:83
  104.0 1.5 broadcast_select_fusion
  105.5 39.2 %psum.30 = f32[]{:T(128)} all-reduce(f32[]{:T(128)} %multiply_reduce_fusion.1), channel_id=1, replica_groups=mesh['grp'=4,'dev'=8] {'grp','dev'}, use_global_device_ids=true, to_apply=%region_6.7 | all-reduce | flops 1 | bytes 8 | tf_op jit(solution)/shard_map/psum | solution.py:83
  145.9 3.2 %multiply_add_fusion.2 = f32[16,32,1024]{2,0,1:T(8,128)S(1)} fusion(f32[]{:T(128)S(6)} %div.34, f32[16,32,1024]{2,0,1:T(8,128)} %get-tuple-element.17, f32[]{:T(128)S(6)} %div.33, f32[16,32,1024]{2,1,0:T(8,128)S(1)} %copy-done), kind=kLoop, calls=%fused_computation.88 | loop fusion | flops 2097152 | bytes 6291464 | tf_op jit(solution)/shard_map/add | solution.py:126
  149.1 1.3 copy-done.1
  150.4 0.2 fusion.45
  150.6 1.3 collective-permute-start.8
  152.0 4.6 %collective-permute-start.9 = (f32[1,32,1024]{2,1,0:T(8,128)S(1)}, f32[1,32,1024]{2,1,0:T(8,128)S(1)}, u32[]{:S(2)}, u32[]{:S(2)}) collective-permute-start(f32[1,32,1024]{2,1,0:T(8,128)S(1)} %copy.78), channel_id=1, source_target_pairs={{0,8},{8,16},{16,24},{1,9},{9,17},{17,25},{2,10},{10,18},{18,26},{... | collective-permute-start | bytes 393224 | tf_op jit(solution)/shard_map/ppermute | solution.py:17
  156.6 2.6 %fusion.5 = f32[16,32,1025]{2,1,0:T(8,128)} fusion(f32[16,32,1026]{2,1,0:T(8,128)S(1)} %copy-done.12, f32[16,32,1024]{2,1,0:T(8,128)S(1)} %copy-done.13, f32[16,32,1024]{2,1,0:T(8,128)S(1)} %copy-done.10), kind=kLoop, calls=%fused_computation.23 | loop fusion | flops 6297600 | bytes 10491904 | tf_op jit(solution)/shard_map/jit(_where)/select_n | solution.py:37
  159.4 0.1 broadcast_in_dim.15
  159.5 0.8 broadcast_in_dim.16
  160.5 0.1 copy.79
  160.6 1.1 pad_maximum_fusion.16
  161.7 1.3 collective-permute-start.10
  163.0 3.2 %collective-permute-start.11 = (f32[18,1,1024]{2,0,1:T(8,128)S(1)}, f32[18,1,1024]{2,0,1:T(8,128)S(1)}, u32[]{:S(2)}, u32[]{:S(2)}) collective-permute-start(f32[18,1,1024]{2,0,1:T(8,128)S(1)} %get-tuple-element.18), channel_id=1, source_target_pairs={{0,1},{1,2},{2,3},{3,4},{4,5},{5,6},{6,7},{8,9},{9,10},{10,11},{11... | collective-permute-start | bytes 221192 | tf_op jit(solution)/shard_map/ppermute | solution.py:17
  166.2 4.6 %fusion.41 = f32[16,32,1024]{2,1,0:T(8,128)} fusion(f32[16,32,1024]{2,1,0:T(8,128)S(1)} %copy-done.11, f32[16,32,1025]{2,1,0:T(8,128)} %fusion.5, pred[32,1024]{1,0:T(8,128)(4,1)S(1)} %broadcast_in_dim.16), kind=kLoop, calls=%fused_computation.84 | loop fusion | flops 2097152 | bytes 8421376 | tf_op jit(solution)/shard_map/jit(_where)/select_n | solution.py:107
  170.8 3.7 %select_maximum_fusion = f32[18,34,1026]{2,0,1:T(8,128)S(1)} fusion(f32[18,1,1024]{2,0,1:T(8,128)S(1)} %collective-permute-done.10, f32[18,1,1024]{2,0,1:T(8,128)S(1)} %collective-permute-done.11, f32[1,32,1024]{2,0,1:T(1,128)S(1)} %copy.77, f32[16,32,1024]{2,0,1:T(8,128)S(1)} %copy-done.2, f32[1,32,1024]{2,0,1:T(1,128)S(1)} %copy.79), kind=kLoop, calls=%fused_computation.2 | loop fusion | flops 7534944 | bytes 5018400 | tf_op jit(solution)/shard_map/concatenate | solution.py:19
  174.6 6.0 %multiply_reduce_fusion = (f32[]{:T(128)}, f32[16,32,1024]{2,0,1:T(8,128)}) fusion(f32[16,32,1024]{2,0,1:T(8,128)S(1)} %copy-done.2, f32[18,34,1026]{2,0,1:T(8,128)S(1)} %select_maximum_fusion, f32[16,32,1025]{2,0,1:T(8,128)S(1)} %copy-done.6, f32[1,32,1024]{2,0,1:T(1,128)S(1)} %copy.77, f32[1,32,1024]{2,0,1:T(1,128)S(1)} %copy.79, ...), kind=kLoop, calls=%fused_computation.87 | loop fusion | flops 14155775 | bytes 21381124 | tf_op jit(solution)/shard_map/reduce_sum | solution.py:122
  180.5 41.6 %psum.31 = f32[]{:T(128)} all-reduce(f32[]{:T(128)} %get-tuple-element.14), channel_id=1, replica_groups=mesh['grp'=4,'dev'=8] {'grp','dev'}, use_global_device_ids=true, to_apply=%region_8.9 | all-reduce | flops 1 | bytes 8 | tf_op jit(solution)/shard_map/psum | solution.py:122
  223.4 4.7 %multiply_subtract_fusion = (f32[16,32,1024]{2,0,1:T(8,128)S(1)}, f32[16,32,1024]{2,0,1:T(8,128)S(1)}) fusion(f32[16,32,1024]{2,0,1:T(8,128)} %get-tuple-element.15, f32[]{:T(128)S(6)} %div.35, f32[16,32,1024]{2,0,1:T(8,128)} %get-tuple-element.17, f32[]{:T(128)S(6)} %div.33, f32[16,32,1024]{2,1,0:T(8,128)S(1)} %copy-done, f32[16,32,1024]{2,0,1:T(8,128)} %copy-done.1), kind=kLoop, calls=%fused_computation.85 | loop fusion | flops 3670016 | bytes 12582920 | tf_op jit(solution)/shard_map/sub | solution.py:124
  228.1 2.5 %copy.82 = f32[16,32,1024]{2,1,0:T(8,128)} copy(f32[16,32,1024]{2,0,1:T(8,128)S(1)} %get-tuple-element.25) | data formatting | bytes 4194304
  230.6 2.5 %copy.83 = f32[16,32,1024]{2,1,0:T(8,128)} copy(f32[16,32,1024]{2,0,1:T(8,128)S(1)} %get-tuple-element.24) | data formatting | bytes 4194304
  (54 shorter events, 0.7 us)
Async XLA Ops:
  0.6 17.0 %copy-start.9 = (f32[16,32,1024]{2,1,0:T(8,128)S(1)}, f32[16,32,1024]{2,1,0:T(8,128)}, u32[]{:S(2)}) copy-start(f32[16,32,1024]{2,1,0:T(8,128)} %param.5) | copy-start | bytes 6291460
  1.8 26.2 %collective-permute-start.4 = (f32[1,32,1024]{2,1,0:T(8,128)S(1)}, f32[1,32,1024]{2,1,0:T(8,128)S(1)}, u32[]{:S(2)}, u32[]{:S(2)}) collective-permute-start(f32[1,32,1024]{2,1,0:T(8,128)S(1)} %get-tuple-element.31), channel_id=1, source_target_pairs={{8,0},{16,8},{24,16},{9,1},{17,9},{25,17},{10,2},{18,10},{26,18},{... | collective-permute-start | bytes 393224 | tf_op jit(solution)/shard_map/ppermute | solution.py:18
  3.1 25.0 %collective-permute-start.5 = (f32[1,32,1024]{2,1,0:T(8,128)S(1)}, f32[1,32,1024]{2,1,0:T(8,128)S(1)}, u32[]{:S(2)}, u32[]{:S(2)}) collective-permute-start(f32[1,32,1024]{2,1,0:T(8,128)S(1)} %get-tuple-element.30), channel_id=1, source_target_pairs={{0,8},{8,16},{16,24},{1,9},{9,17},{17,25},{2,10},{10,18},{18,26},{... | collective-permute-start | bytes 393224 | tf_op jit(solution)/shard_map/ppermute | solution.py:17
  9.7 15.3 %collective-permute-start = (f32[1,32,1024]{2,1,0:T(8,128)S(1)}, f32[1,32,1024]{2,1,0:T(8,128)S(1)}, u32[]{:S(2)}, u32[]{:S(2)}) collective-permute-start(f32[1,32,1024]{2,1,0:T(8,128)S(1)} %get-tuple-element.28), channel_id=1, source_target_pairs={{0,8},{8,16},{16,24},{1,9},{9,17},{17,25},{2,10},{10,18},{18,26},{... | collective-permute-start | bytes 393224 | tf_op jit(solution)/shard_map/ppermute | solution.py:17
  13.6 11.5 %collective-permute-start.1 = (f32[1,32,1024]{2,1,0:T(8,128)S(1)}, f32[1,32,1024]{2,1,0:T(8,128)S(1)}, u32[]{:S(2)}, u32[]{:S(2)}) collective-permute-start(f32[1,32,1024]{2,1,0:T(8,128)S(1)} %get-tuple-element.29), channel_id=1, source_target_pairs={{8,0},{16,8},{24,16},{9,1},{17,9},{25,17},{10,2},{18,10},{26,18},{... | collective-permute-start | bytes 393224 | tf_op jit(solution)/shard_map/ppermute | solution.py:18
  18.9 3.0 %copy-start.15 = (f32[2]{0:T(128)S(1)}, f32[2]{0:T(128)}, u32[]{:S(2)}) copy-start(f32[2]{0:T(128)} %param.8) | copy-start | bytes 28
  18.9 3.6 %copy-start = (f32[16,32,1024]{2,1,0:T(8,128)S(1)}, f32[16,32,1024]{2,1,0:T(8,128)}, u32[]{:S(2)}) copy-start(f32[16,32,1024]{2,1,0:T(8,128)} %param.7) | copy-start | bytes 6291460
  25.3 9.8 %collective-permute-start.2 = (f32[18,1,1024]{2,0,1:T(8,128)S(1)}, f32[18,1,1024]{2,0,1:T(8,128)S(1)}, u32[]{:S(2)}, u32[]{:S(2)}) collective-permute-start(f32[18,1,1024]{2,0,1:T(8,128)S(1)} %get-tuple-element.20), channel_id=1, source_target_pairs={{0,1},{1,2},{2,3},{3,4},{4,5},{5,6},{6,7},{8,9},{9,10},{10,11},{11... | collective-permute-start | bytes 221192 | tf_op jit(solution)/shard_map/ppermute | solution.py:17
  26.6 8.5 %collective-permute-start.3 = (f32[18,1,1024]{2,0,1:T(8,128)S(1)}, f32[18,1,1024]{2,0,1:T(8,128)S(1)}, u32[]{:S(2)}, u32[]{:S(2)}) collective-permute-start(f32[18,1,1024]{2,0,1:T(8,128)S(1)} %get-tuple-element.21), channel_id=1, source_target_pairs={{1,0},{2,1},{3,2},{4,3},{5,4},{6,5},{7,6},{9,8},{10,9},{11,10},{12... | collective-permute-start | bytes 221192 | tf_op jit(solution)/shard_map/ppermute | solution.py:18
  28.3 15.9 %collective-permute-start.6 = (f32[18,1,1024]{2,0,1:T(8,128)S(1)}, f32[18,1,1024]{2,0,1:T(8,128)S(1)}, u32[]{:S(2)}, u32[]{:S(2)}) collective-permute-start(f32[18,1,1024]{2,0,1:T(8,128)S(1)} %get-tuple-element.23), channel_id=1, source_target_pairs={{1,0},{2,1},{3,2},{4,3},{5,4},{6,5},{7,6},{9,8},{10,9},{11,10},{12... | collective-permute-start | bytes 221192 | tf_op jit(solution)/shard_map/ppermute | solution.py:18
  29.6 14.6 %collective-permute-start.7 = (f32[18,1,1024]{2,0,1:T(8,128)S(1)}, f32[18,1,1024]{2,0,1:T(8,128)S(1)}, u32[]{:S(2)}, u32[]{:S(2)}) collective-permute-start(f32[18,1,1024]{2,0,1:T(8,128)S(1)} %get-tuple-element.22), channel_id=1, source_target_pairs={{0,1},{1,2},{2,3},{3,4},{4,5},{5,6},{6,7},{8,9},{9,10},{10,11},{11... | collective-permute-start | bytes 221192 | tf_op jit(solution)/shard_map/ppermute | solution.py:17
  42.1 5.8 %copy-start.7 = (f32[17,32,1024]{2,0,1:T(8,128)}, f32[17,32,1024]{2,0,1:T(8,128)S(1)}, u32[]{:S(2)}) copy-start(f32[17,32,1024]{2,0,1:T(8,128)S(1)} %fusion.1) | copy-start | bytes 6684676
  42.9 5.0 %copy-start.5 = (f32[16,32,1025]{2,0,1:T(8,128)}, f32[16,32,1025]{2,0,1:T(8,128)S(1)}, u32[]{:S(2)}) copy-start(f32[16,32,1025]{2,0,1:T(8,128)S(1)} %fusion.2) | copy-start | bytes 6297604
  44.2 3.7 %copy-start.3 = (f32[16,33,1024]{2,0,1:T(8,128)}, f32[16,33,1024]{2,0,1:T(8,128)S(1)}, u32[]{:S(2)}) copy-start(f32[16,33,1024]{2,0,1:T(8,128)S(1)} %fusion.8) | copy-start | bytes 6488068
  100.4 3.5 %copy-start.14 = (f32[16,32,1024]{2,1,0:T(8,128)S(1)}, f32[16,32,1024]{2,1,0:T(8,128)}, u32[]{:S(2)}) copy-start(f32[16,32,1024]{2,1,0:T(8,128)} %param.6) | copy-start | bytes 6291460
  145.9 10.7 %copy-start.10 = (f32[16,32,1024]{2,1,0:T(8,128)S(1)}, f32[16,32,1024]{2,1,0:T(8,128)}, u32[]{:S(2)}) copy-start(f32[16,32,1024]{2,1,0:T(8,128)} %param.5) | copy-start | bytes 6291460
  145.9 10.7 %copy-start.12 = (f32[16,32,1026]{2,1,0:T(8,128)S(1)}, f32[16,32,1026]{2,1,0:T(8,128)}, u32[]{:S(2)}) copy-start(f32[16,32,1026]{2,1,0:T(8,128)} %minimum_multiply_fusion) | copy-start | bytes 6303748
  145.9 10.7 %copy-start.13 = (f32[16,32,1024]{2,1,0:T(8,128)S(1)}, f32[16,32,1024]{2,1,0:T(8,128)}, u32[]{:S(2)}) copy-start(f32[16,32,1024]{2,1,0:T(8,128)} %broadcast_select_fusion) | copy-start | bytes 6291460
  149.1 1.3 copy-start.1
  150.6 9.7 %collective-permute-start.8 = (f32[1,32,1024]{2,1,0:T(8,128)S(1)}, f32[1,32,1024]{2,1,0:T(8,128)S(1)}, u32[]{:S(2)}, u32[]{:S(2)}) collective-permute-start(f32[1,32,1024]{2,1,0:T(8,128)S(1)} %copy.76), channel_id=1, source_target_pairs={{8,0},{16,8},{24,16},{9,1},{17,9},{25,17},{10,2},{18,10},{26,18},{... | collective-permute-start | bytes 393224 | tf_op jit(solution)/shard_map/ppermute | solution.py:18
  152.0 7.2 %copy-start.16 = (s32[1,1,128]{2,1,0:T(1,128)S(1)}, s32[1,1,128]{2,1,0:T(1,128)}, u32[]{:S(2)}) copy-start(s32[1,1,128]{2,1,0:T(1,128)} %param.9) | copy-start | bytes 1540
  152.0 8.5 %collective-permute-start.9 = (f32[1,32,1024]{2,1,0:T(8,128)S(1)}, f32[1,32,1024]{2,1,0:T(8,128)S(1)}, u32[]{:S(2)}, u32[]{:S(2)}) collective-permute-start(f32[1,32,1024]{2,1,0:T(8,128)S(1)} %copy.78), channel_id=1, source_target_pairs={{0,8},{8,16},{16,24},{1,9},{9,17},{17,25},{2,10},{10,18},{18,26},{... | collective-permute-start | bytes 393224 | tf_op jit(solution)/shard_map/ppermute | solution.py:17
  160.3 5.9 %copy-start.11 = (f32[16,32,1024]{2,1,0:T(8,128)S(1)}, f32[16,32,1024]{2,1,0:T(8,128)}, u32[]{:S(2)}) copy-start(f32[16,32,1024]{2,1,0:T(8,128)} %param.5) | copy-start | bytes 6291460
  161.7 9.1 %collective-permute-start.10 = (f32[18,1,1024]{2,0,1:T(8,128)S(1)}, f32[18,1,1024]{2,0,1:T(8,128)S(1)}, u32[]{:S(2)}, u32[]{:S(2)}) collective-permute-start(f32[18,1,1024]{2,0,1:T(8,128)S(1)} %get-tuple-element.19), channel_id=1, source_target_pairs={{1,0},{2,1},{3,2},{4,3},{5,4},{6,5},{7,6},{9,8},{10,9},{11,10},{12... | collective-permute-start | bytes 221192 | tf_op jit(solution)/shard_map/ppermute | solution.py:18
  163.0 7.8 %copy-start.2 = (f32[16,32,1024]{2,0,1:T(8,128)S(1)}, f32[16,32,1024]{2,0,1:T(8,128)}, u32[]{:S(2)}) copy-start(f32[16,32,1024]{2,0,1:T(8,128)} %copy-done.1) | copy-start | bytes 6291460
  163.0 7.8 %collective-permute-start.11 = (f32[18,1,1024]{2,0,1:T(8,128)S(1)}, f32[18,1,1024]{2,0,1:T(8,128)S(1)}, u32[]{:S(2)}, u32[]{:S(2)}) collective-permute-start(f32[18,1,1024]{2,0,1:T(8,128)S(1)} %get-tuple-element.18), channel_id=1, source_target_pairs={{0,1},{1,2},{2,3},{3,4},{4,5},{5,6},{6,7},{8,9},{9,10},{10,11},{11... | collective-permute-start | bytes 221192 | tf_op jit(solution)/shard_map/ppermute | solution.py:17
  166.2 8.4 %copy-start.8 = (f32[17,32,1024]{2,0,1:T(8,128)S(1)}, f32[17,32,1024]{2,0,1:T(8,128)}, u32[]{:S(2)}) copy-start(f32[17,32,1024]{2,0,1:T(8,128)} %copy-done.7) | copy-start | bytes 6684676
  170.8 3.7 %copy-start.4 = (f32[16,33,1024]{2,0,1:T(8,128)S(1)}, f32[16,33,1024]{2,0,1:T(8,128)}, u32[]{:S(2)}) copy-start(f32[16,33,1024]{2,0,1:T(8,128)} %copy-done.3) | copy-start | bytes 6488068
  170.8 3.7 %copy-start.6 = (f32[16,32,1025]{2,0,1:T(8,128)S(1)}, f32[16,32,1025]{2,0,1:T(8,128)}, u32[]{:S(2)}) copy-start(f32[16,32,1025]{2,0,1:T(8,128)} %copy-done.5) | copy-start | bytes 6297604
where the time goes:
time: 234 us; the launch traced here: 233 us
  blocking collectives  124 us (53%)
  other arithmetic  58.7 us (25%)
  starting transfers between devices  31.8 us (14%)
  local copies, waits for them, and re-layouts  13.7 us (6%)
  between operations  5.04 us (2%)
    psum x2, blocking collectives, squares(): return lax.psum(jnp.sum(residual * residual), ('grp', 'dev'))  82.2 us
    psum x1, blocking collectives, on_device(): lax.psum(jnp.sum(direction * image_vec), ('grp', 'dev'))  41.6 us
    ppermute x6, starting transfers between devices, with_halo(): before = lax.ppermute(last, axis, up)  24.1 us
    reduce_sum x2, other arithmetic, on_device(): jnp.sum(direction * image_vec)  14.1 us
    unnamed x38, local copies, waits for them, and re-layouts  8.88 us
    concatenate x4, other arithmetic, with_halo(): value = jnp.concatenate([before, value, after], axis=dim)  8.47 us
    ppermute x6, starting transfers between devices, with_halo(): after = lax.ppermute(first, axis, down)  7.75 us
    reduce_sum x2, other arithmetic, squares(): return lax.psum(jnp.sum(residual * residual), ('grp', 'dev'))  6.27 us
  transfers between devices with their start and end apart: 12, of which 0 were waited for; matrix products, arithmetic and copies ran while one was open for 12% of the time, Pallas kernels for 0%

commit v1 on v0

v1 whole, which is shorter than its diff:
```python
import functools

import jax
import jax.numpy as jnp
from jax import lax
from jax.experimental import pallas as pl
from jax.experimental.pallas import tpu as pltpu
from jax.sharding import PartitionSpec as P

TILE = 16
SUB = 8
LANES = 128
MESH = pl.DeviceIdType.MESH


def fold(value):
    total = value[:, 0:LANES]
    for start in range(LANES, value.shape[1], LANES):
        total = total + value[:, start : start + LANES]
    return total


def kernel(
    sizes,
    frac_in,
    cour_in,
    div_in,
    dens,
    band,
    frac_out,
    pres_out,
    res_out,
    frac,
    cour,
    field,
    image,
    second,
    beta0,
    beta1,
    beta2,
    beta_last,
    mask,
    row_send,
    row_recv,
    sum_grp,
    sum_dev,
    load_sem,
    plane_send_sem,
    plane_recv_sem,
    row_send_sem,
    row_recv_sem,
    grp_send_sem,
    grp_recv_sem,
    dev_send_sem,
    dev_recv_sem,
):
    groups, devs = sizes
    depth, rows, width = frac_in.shape
    blocks = rows // SUB
    g = lax.axis_index("grp")
    d = lax.axis_index("dev")
    inner = pl.ds(SUB, rows)

    loads = []
    for slot, (source, target) in enumerate(
        (
            (frac_in, frac.at[pl.ds(1, depth), inner]),
            (div_in, field.at[pl.ds(1, depth), inner]),
            (cour_in, cour),
        )
    ):
        copy = pltpu.make_async_copy(source, target, load_sem.at[slot])
        copy.start()
        loads.append(copy)

    barrier = pltpu.get_barrier_semaphore()
    for step in range(1, groups):
        pl.semaphore_signal(
            barrier, inc=1, device_id={"grp": lax.rem(g + step, groups)}, device_id_type=MESH
        )
    for step in range(1, devs):
        pl.semaphore_signal(
            barrier, inc=1, device_id={"dev": lax.rem(d + step, devs)}, device_id_type=MESH
        )

    padded = (frac, field, image)
    edges = ((g > 0, g == 0), (g < groups - 1, g == groups - 1))
    row_edges = ((d > 0, d == 0), (d < devs - 1, d == devs - 1))

    for side in range(2):
        plane = 0 if side == 0 else depth + 1

        @pl.when(edges[side][1])
        def _():
            for target in padded:
                target[plane, inner, :] = jnp.zeros((rows, width), jnp.float32)

        @pl.when(row_edges[side][1])
        def _():
            for which in range(3):
                row_recv[which, side] = jnp.zeros((depth, width), jnp.float32)

    across = rows // TILE
    along = width // TILE
    ids = (
        lax.broadcasted_iota(jnp.int32, (SUB, width), 1) // TILE
        + lax.broadcasted_iota(jnp.int32, (SUB, width), 0) * along
    )

    def listed(entry, seen):
        return jnp.where(ids == band[entry], 1.0, seen)

    mask[...] = lax.fori_loop(
        0, across * along, listed, jnp.zeros((SUB, width), jnp.float32)
    )

    pl.semaphore_wait(barrier, groups + devs - 2)

    def plane_copy(which, source, side):
        target = padded[which]
        plane = depth + 1 if side == 0 else 0
        other = lax.rem(g + (groups - 1 if side == 0 else 1), groups)
        return pltpu.make_async_remote_copy(
            src_ref=source,
            dst_ref=target.at[plane, inner],
            send_sem=plane_send_sem.at[which, side],
            recv_sem=plane_recv_sem.at[which, 1 - side],
            device_id={"grp": other},
            device_id_type=MESH,
        )

    def row_copy(which, side):
        other = lax.rem(d + (devs - 1 if side == 0 else 1), devs)
        return pltpu.make_async_remote_copy(
            src_ref=row_send.at[which, side],
            dst_ref=row_recv.at[which, 1 - side],
            send_sem=row_send_sem.at[which, side],
            recv_sem=row_recv_sem.at[which, 1 - side],
            device_id={"dev": other},
            device_id_type=MESH,
        )

    def plane_source(which, side):
        plane = 0 if side == 0 else depth - 1
        if which == 2:
            return image.at[plane + 1, inner]
        return (frac_in, div_in)[which].at[plane]

    def send_planes(which):
        for side in range(2):

            @pl.when(edges[side][0])
            def _():
                plane_copy(which, plane_source(which, side), side).start()

    def send_rows(which):
        source = padded[which]

        def pack(i, carry):
            row_send[which, 0, pl.ds(i, 1), :] = source[i + 1, pl.ds(SUB, 1), :]
            row_send[which, 1, pl.ds(i, 1), :] = source[i + 1, pl.ds(SUB + rows - 1, 1), :]
            return carry

        lax.fori_loop(0, depth, pack, 0)
        for side in range(2):

            @pl.when(row_edges[side][0])
            def _():
                row_copy(which, side).start()

    def receive(which):
        for side in range(2):

            @pl.when(row_edges[side][0])
            def _():
                row_copy(which, side).wait_send()
                row_copy(which, 1 - side).wait_recv()

        target = padded[which]

        def unpack(i, carry):
            target[i + 1, pl.ds(SUB - 1, 1), :] = row_recv[which, 0, pl.ds(i, 1), :]
            target[i + 1, pl.ds(SUB + rows, 1), :] = row_recv[which, 1, pl.ds(i, 1), :]
            return carry

        lax.fori_loop(0, depth, unpack, 0)
        for side in range(2):

            @pl.when(edges[side][0])
            def _():
                plane_copy(which, plane_source(which, side), side).wait_send()
                plane_copy(which, plane_source(which, 1 - side), 1 - side).wait_recv()

    send_planes(0)
    send_planes(1)
    loads[0].wait()
    send_rows(0)
    loads[1].wait()
    send_rows(1)

    half0 = 0.5 * dens[0]
    half1 = 0.5 * dens[1]

    def half_density(value):
        return value * half0 + (1.0 - value) * half1

    lane = lax.broadcasted_iota(jnp.int32, (SUB, width), 1)
    first_lane = lane == 0
    last_lane = lane == width - 1
    tail = pl.ds(width - LANES, LANES)

    def chunk(block, offset=0):
        return pl.ds(SUB + block * SUB + offset, SUB)

    def local_betas(i, carry):
        for block in range(blocks):
            own = half_density(frac[i + 1, chunk(block), :])
            below = jnp.where(first_lane, half1, pltpu.roll(own, 1, 1))
            here = pl.ds(block * SUB, SUB)
            beta2[i, here, :] = 1.0 / (own + below)
            beta_last[i, here, :] = 1.0 / (own[:, width - LANES :] + half1)
        return carry

    lax.fori_loop(0, depth, local_betas, 0)

    def first_faces(i):
        for block in range(blocks):
            own = half_density(frac[i + 1, chunk(block), :])
            before = half_density(frac[i, chunk(block), :])
            beta0[i, pl.ds(block * SUB, SUB), :] = 1.0 / (own + before)

    def first_betas(i, carry):
        first_faces(i)
        return carry

    lax.fori_loop(1, depth, first_betas, 0)

    receive(0)
    first_faces(0)
    first_faces(depth)

    def second_betas(i, carry):
        for block in range(blocks):
            own = half_density(frac[i + 1, chunk(block), :])
            before = half_density(frac[i + 1, chunk(block, -1), :])
            beta1[i, pl.ds(block * SUB, SUB), :] = 1.0 / (own + before)
        own = half_density(frac[i + 1, pl.ds(SUB + rows, 1), :])
        before = half_density(frac[i + 1, pl.ds(SUB + rows - 1, 1), :])
        beta1[i, pl.ds(rows, 1), :] = 1.0 / (own + before)
        return carry

    lax.fori_loop(0, depth, second_betas, 0)

    receive(1)

    def operator(source, i, block):
        here = pl.ds(block * SUB, SUB)
        own = source[i + 1, chunk(block), :]
        result = beta0[i + 1, here, :] * (own - source[i + 2, chunk(block), :])
        result = result + beta0[i, here, :] * (own - source[i, chunk(block), :])
        result = result + beta1[i, pl.ds(block * SUB + 1, SUB), :] * (
            own - source[i + 1, chunk(block, 1), :]
        )
        result = result + beta1[i, here, :] * (own - source[i + 1, chunk(block, -1), :])
        below = jnp.where(first_lane, 0.0, pltpu.roll(own, 1, 1))
        low = beta2[i, here, :] * (own - below)
        end = beta_last[i, here, :] * own[:, width - LANES :]
        end = jnp.concatenate([low[:, : width - LANES], end], axis=1)
        high = jnp.where(last_lane, -end, pltpu.roll(low, width - 1, 1))
        return own, result + (low - high)

    def first_image(i, carry):
        norm, cross = carry
        for block in range(blocks):
            own, result = operator(field, i, block)
            image[i + 1, chunk(block), :] = result
            norm = norm + fold(own * own)
            cross = cross + fold(own * result)
        return norm, cross

    nothing = jnp.zeros((SUB, LANES), jnp.float32)
    norm, cross = lax.fori_loop(0, depth, first_image, (nothing, nothing))

    unit = lax.broadcasted_iota(jnp.int32, (1, LANES), 1)

    def message(parts):
        value = jnp.zeros((1, LANES), jnp.float32)
        for place, part in enumerate(parts):
            value = jnp.where(unit == place, jnp.sum(part), value)
        return value

    def stage(phase, axis, buffer, send_sem, recv_sem, index, count):
        def copy(step):
            return pltpu.make_async_remote_copy(
                src_ref=buffer.at[phase, index],
                dst_ref=buffer.at[phase, index],
                send_sem=send_sem.at[phase, step],
                recv_sem=recv_sem.at[phase, step],
                device_id={axis: lax.rem(index + step, count)},
                device_id_type=MESH,
            )

        def start(value):
            buffer[phase, pl.ds(index, 1)] = value.reshape(1, 1, LANES)
            for step in range(1, count):
                copy(step).start()

        def finish():
            for step in range(1, count):
                copy(step).wait()
            total = buffer[phase, 0]
            for other in range(1, count):
                total = total + buffer[phase, other]
            return total

        return start, finish

    def across_grp(phase):
        return stage(phase, "grp", sum_grp, grp_send_sem, grp_recv_sem, g, groups)

    def across_dev(phase):
        return stage(phase, "dev", sum_dev, dev_send_sem, dev_recv_sem, d, devs)

    def pick(total, place):
        return jnp.sum(jnp.where(unit == place, total, 0.0), axis=1, keepdims=True)

    send_planes(2)
    start_grp, finish_grp = across_grp(0)
    start_grp(message((norm, cross)))
    send_rows(2)

    loads[2].wait()

    def advect(i, carry):
        for block in range(blocks):
            own = frac[i + 1, chunk(block), :]
            speed = jnp.where(first_lane, 0.0, cour[i, pl.ds(block * SUB, SUB), :])
            left = jnp.where(first_lane, 0.0, pltpu.roll(own, 1, 1))
            behind = own - left
            ahead = jnp.where(last_lane, -own, pltpu.roll(behind, width - 1, 1))
            slope = jnp.maximum(0.0, jnp.minimum(ahead, behind)) + jnp.minimum(
                0.0, jnp.maximum(ahead, behind)
            )
            forward = speed > 0
            upwind = jnp.where(forward, left, own)
            tilt = jnp.where(forward, pltpu.roll(slope, 1, 1), -slope)
            flux = speed * (upwind + 0.5 * (1.0 - jnp.abs(speed)) * tilt)
            moved = jnp.clip(own - (pltpu.roll(flux, width - 1, 1) - flux), 0.0, 1.0)
            flag = mask[pl.ds(block * SUB // TILE, 1), :]
            frac_out[i, pl.ds(block * SUB, SUB), :] = jnp.where(flag > 0.5, moved, own)
        return carry

    half_way = depth // 2
    lax.fori_loop(0, half_way, advect, 0)
    start_dev, finish_dev = across_dev(0)
    start_dev(finish_grp())
    lax.fori_loop(half_way, depth, advect, 0)

    receive(2)

    def second_image(i, carry):
        for block in range(blocks):
            own, result = operator(image, i, block)
            second[i, pl.ds(block * SUB, SUB), :] = result
        return carry

    lax.fori_loop(0, depth, second_image, 0)

    total = finish_dev()
    norm0 = pick(total, 0)
    cross0 = pick(total, 1)
    alpha0 = norm0 / cross0

    def moments(i, carry):
        norm, mixed, cross = carry
        for block in range(blocks):
            here = pl.ds(block * SUB, SUB)
            ahead = image[i + 1, chunk(block), :]
            left = field[i + 1, chunk(block), :] - alpha0 * ahead
            norm = norm + fold(left * left)
            mixed = mixed + fold(left * ahead)
            cross = cross + fold(left * (ahead - alpha0 * second[i, here, :]))
        return norm, mixed, cross

    sums = lax.fori_loop(0, depth, moments, (nothing, nothing, nothing))
    start_grp, finish_grp = across_grp(1)
    start_grp(message(sums))
    start_dev, finish_dev = across_dev(1)
    start_dev(finish_grp())
    total = finish_dev()
    norm1 = pick(total, 0)
    mixed1 = pick(total, 1)
    cross1 = pick(total, 2)
    ratio = norm1 / norm0
    alpha1 = norm1 / (cross1 + ratio * (2.0 * mixed1 + ratio * cross0))

    def finish(i, carry):
        for block in range(blocks):
            here = pl.ds(block * SUB, SUB)
            begin = field[i + 1, chunk(block), :]
            ahead = image[i + 1, chunk(block), :]
            left = begin - alpha0 * ahead
            pres_out[i, here, :] = alpha0 * begin + alpha1 * (left + ratio * begin)
            res_out[i, here, :] = left - alpha1 * (
                (ahead - alpha0 * second[i, here, :]) + ratio * ahead
            )
        return carry

    lax.fori_loop(0, depth, finish, 0)


def on_device(sizes, fraction, courant, divergence, densities, band_tiles):
    depth, rows, width = fraction.shape
    groups, devs = sizes
    padded = pltpu.VMEM((depth + 2, rows + 2 * SUB, width), jnp.float32)
    plain = pltpu.VMEM((depth, rows, width), jnp.float32)
    shape = jax.ShapeDtypeStruct((depth, rows, width), jnp.float32)
    return pl.pallas_call(
        functools.partial(kernel, sizes),
        out_shape=(shape, shape, shape),
        in_specs=[pl.BlockSpec(memory_space=pl.ANY)] * 3
        + [pl.BlockSpec(memory_space=pltpu.SMEM)] * 2,
        out_specs=[pl.BlockSpec(memory_space=pltpu.VMEM)] * 3,
        scratch_shapes=[
            padded,
            plain,
            padded,
            padded,
            plain,
            pltpu.VMEM((depth + 1, rows, width), jnp.float32),
            pltpu.VMEM((depth, rows + SUB, width), jnp.float32),
            plain,
            pltpu.VMEM((depth, rows, LANES), jnp.float32),
            pltpu.VMEM((SUB, width), jnp.float32),
            pltpu.VMEM((3, 2, depth, width), jnp.float32),
            pltpu.VMEM((3, 2, depth, width), jnp.float32),
            pltpu.VMEM((2, groups, 1, LANES), jnp.float32),
            pltpu.VMEM((2, devs, 1, LANES), jnp.float32),
            pltpu.SemaphoreType.DMA((3,)),
            pltpu.SemaphoreType.DMA((3, 2)),
            pltpu.SemaphoreType.DMA((3, 2)),
            pltpu.SemaphoreType.DMA((3, 2)),
            pltpu.SemaphoreType.DMA((3, 2)),
            pltpu.SemaphoreType.DMA((2, groups)),
            pltpu.SemaphoreType.DMA((2, groups)),
            pltpu.SemaphoreType.DMA((2, devs)),
            pltpu.SemaphoreType.DMA((2, devs)),
        ],
        compiler_params=pltpu.CompilerParams(
            collective_id=0, has_side_effects=True, vmem_limit_bytes=60 * 1024 * 1024
        ),
    )(fraction, courant, divergence, densities, band_tiles.reshape(-1))


def solution(mesh):
    sizes = (mesh.shape["grp"], mesh.shape["dev"])
    placed = P("grp", "dev", None)
    return jax.shard_map(
        functools.partial(on_device, sizes),
        mesh=mesh,
        in_specs=(placed, placed, placed, P(), placed),
        out_specs=(placed, placed, placed),
        check_vma=False,
    )
```

time: 234 us -> 47.5 us (0.20)
  blocking collectives: 124 us -> 0 us
  other arithmetic: 58.7 us -> 0 us
  Pallas kernels: 0 us -> 39.7 us
  starting transfers between devices: 31.8 us -> 0 us
  local copies, waits for them, and re-layouts: 13.7 us -> 6.98 us
  between operations: 5.04 us -> 0.65 us
    psum x3 -> x0, blocking collectives: 124 us -> none  [the longest x2 82.2 us: squares(): return lax.psum(jnp.sum(residual * residual), ('grp', 'dev'))]
    pallas_call x0 -> x1, Pallas kernels: none -> 39.7 us  [on_device(): pl.pallas_call(functools.partial(kernel, sizes), out_shape=(shape, shape,...]
    ppermute x12 -> x0, starting transfers between devices: 31.8 us -> none  [the longest x6 24.1 us: with_halo(): before = lax.ppermute(last, axis, up)]
    reduce_sum x4 -> x0, other arithmetic: 20.3 us -> none  [the longest x2 14.1 us: on_device(): jnp.sum(direction * image_vec)]
    select_n x3 -> x0, other arithmetic: 8.72 us -> none  [the longest x1 4.62 us: on_device(): new_fraction = jnp.where(in_band, advected, fraction)]
    concatenate x4 -> x0, other arithmetic: 8.47 us -> none  [with_halo(): value = jnp.concatenate([before, value, after], axis=dim)]
    add x2 -> x0, other arithmetic: 8.09 us -> none  [the longest x1 4.94 us: on_device(): density = outer * densities[0] + (1.0 - outer) * densities[1]]
    sub x2 -> x0, other arithmetic: 6.01 us -> none  [the longest x1 4.73 us: on_device(): residual = residual - step_length * image_vec]
  transfers between devices with their start and end apart: 12 -> 0, of which waited for: 0 -> 0; matrix products, arithmetic and copies ran while one was open for 12% -> 0% of each run, Pallas kernels for 0% -> 0%
where the time goes in v1:
time: 47.5 us; the launch traced here: 47.4 us
  Pallas kernels  39.7 us (84%)
  local copies, waits for them, and re-layouts  6.98 us (15%)
  between operations  0.65 us (1%)
    pallas_call x1, Pallas kernels, on_device(): pl.pallas_call(functools.partial(kernel, sizes), out_shape=(shape, shape,...  39.7 us
    unnamed x7, local copies, waits for them, and re-layouts  6.98 us

profile of v1, /device:TPU:0, one launch (start us, length us, event | category | flops | bytes accessed | tf_op | source)
XLA Modules:
  0.0 47.4 jit_solution(333784070274891443)
XLA Ops:
  0.6 39.7 %shard_map.76 = (f32[16,32,1024]{2,1,0:T(8,128)}, f32[16,32,1024]{2,1,0:T(8,128)}, f32[16,32,1024]{2,1,0:T(8,128)}) custom-call(f32[16,32,1024]{2,1,0:T(8,128)} %frac_in.1, f32[16,32,1024]{2,1,0:T(8,128)} %cour_in.1, f32[16,32,1024]{2,1,0:T(8,128)} %div_in.1, f32[2]{0:T(128)} %dens.1, s32[128]{0:T(128)} %bitcast.1), custom_call_target="tpu_custom_call" | custom-call | tf_op jit(solution)/shard_map/pallas_call | solution.py:418
  40.4 0.0 copy-start.1
  40.4 3.3 %copy.11 = f32[16,32,1024]{2,1,0:T(8,128)} copy(f32[16,32,1024]{2,1,0:T(8,128)} %get-tuple-element.6) | data formatting | bytes 4194304
  43.7 0.0 copy-done.1
  43.7 0.0 copy-start
  43.7 1.3 %copy.12 = f32[16,32,1024]{2,1,0:T(8,128)} copy(f32[16,32,1024]{2,1,0:T(8,128)S(1)} %copy-done.1) | data formatting | bytes 4194304
  45.0 1.0 %copy-done = f32[16,32,1024]{2,1,0:T(8,128)S(1)} copy-done((f32[16,32,1024]{2,1,0:T(8,128)S(1)}, f32[16,32,1024]{2,1,0:T(8,128)}, u32[]{:S(2)}) %copy-start) | copy-done | bytes 2097176
  46.1 1.3 %copy.13 = f32[16,32,1024]{2,1,0:T(8,128)} copy(f32[16,32,1024]{2,1,0:T(8,128)S(1)} %copy-done) | data formatting | bytes 4194304
Async XLA Ops:
  40.4 3.3 %copy-start.1 = (f32[16,32,1024]{2,1,0:T(8,128)S(1)}, f32[16,32,1024]{2,1,0:T(8,128)}, u32[]{:S(2)}) copy-start(f32[16,32,1024]{2,1,0:T(8,128)} %get-tuple-element.7) | copy-start | bytes 6291460
  43.7 2.3 %copy-start = (f32[16,32,1024]{2,1,0:T(8,128)S(1)}, f32[16,32,1024]{2,1,0:T(8,128)}, u32[]{:S(2)}) copy-start(f32[16,32,1024]{2,1,0:T(8,128)} %get-tuple-element.8) | copy-start | bytes 6291460

commit v2 on v1

v2 whole, which is shorter than its diff:
```python
import functools

import jax
import jax.numpy as jnp
from jax import lax
from jax.experimental import pallas as pl
from jax.experimental.pallas import tpu as pltpu
from jax.sharding import PartitionSpec as P

TILE = 16
SUB = 8
LANES = 128
MIB = 1024 * 1024
MESH = pl.DeviceIdType.MESH


def fold(value):
    total = value[:, 0:LANES]
    for start in range(LANES, value.shape[1], LANES):
        total = total + value[:, start : start + LANES]
    return total


def kernel(
    sizes,
    frac_in,
    cour_in,
    div_in,
    dens,
    band,
    moved,
    field,
    image,
    second,
    factors,
    frac,
    cour,
    beta0,
    beta1,
    beta2,
    beta_last,
    beta_top,
    mask,
    plane_recv,
    row_send,
    row_recv,
    sum_grp,
    sum_dev,
    load_sem,
    plane_send_sem,
    plane_recv_sem,
    row_send_sem,
    row_recv_sem,
    grp_send_sem,
    grp_recv_sem,
    dev_send_sem,
    dev_recv_sem,
):
    groups, devs = sizes
    depth, rows, width = frac_in.shape
    blocks = rows // SUB
    g = lax.axis_index("grp")
    d = lax.axis_index("dev")

    loads = []
    for slot, (source, target) in enumerate(
        ((frac_in, frac), (div_in, field), (cour_in, cour))
    ):
        copy = pltpu.make_async_copy(source, target, load_sem.at[slot])
        copy.start()
        loads.append(copy)

    barrier = pltpu.get_barrier_semaphore()
    for step in range(1, groups):
        pl.semaphore_signal(
            barrier, inc=1, device_id={"grp": lax.rem(g + step, groups)}, device_id_type=MESH
        )
    for step in range(1, devs):
        pl.semaphore_signal(
            barrier, inc=1, device_id={"dev": lax.rem(d + step, devs)}, device_id_type=MESH
        )

    fields = (frac, field, image)
    edges = ((g > 0, g == 0), (g < groups - 1, g == groups - 1))
    row_edges = ((d > 0, d == 0), (d < devs - 1, d == devs - 1))

    for side in range(2):

        @pl.when(edges[side][1])
        def _():
            for which in range(3):
                plane_recv[which, side] = jnp.zeros((rows, width), jnp.float32)

        @pl.when(row_edges[side][1])
        def _():
            for which in range(3):
                row_recv[which, side] = jnp.zeros((depth, width), jnp.float32)

    across = rows // TILE
    along = width // TILE
    ids = (
        lax.broadcasted_iota(jnp.int32, (SUB, width), 1) // TILE
        + lax.broadcasted_iota(jnp.int32, (SUB, width), 0) * along
    )

    def listed(entry, seen):
        return jnp.where(ids == band[entry], 1.0, seen)

    mask[...] = lax.fori_loop(
        0, across * along, listed, jnp.zeros((SUB, width), jnp.float32)
    )

    pl.semaphore_wait(barrier, groups + devs - 2)

    def plane_copy(which, side):
        plane = 0 if side == 0 else depth - 1
        source = (frac_in, div_in, image)[which]
        other = lax.rem(g + (groups - 1 if side == 0 else 1), groups)
        return pltpu.make_async_remote_copy(
            src_ref=source.at[plane],
            dst_ref=plane_recv.at[which, 1 - side],
            send_sem=plane_send_sem.at[which, side],
            recv_sem=plane_recv_sem.at[which, 1 - side],
            device_id={"grp": other},
            device_id_type=MESH,
        )

    def row_copy(which, side):
        other = lax.rem(d + (devs - 1 if side == 0 else 1), devs)
        return pltpu.make_async_remote_copy(
            src_ref=row_send.at[which, side],
            dst_ref=row_recv.at[which, 1 - side],
            send_sem=row_send_sem.at[which, side],
            recv_sem=row_recv_sem.at[which, 1 - side],
            device_id={"dev": other},
            device_id_type=MESH,
        )

    def send_planes(which):
        for side in range(2):

            @pl.when(edges[side][0])
            def _():
                plane_copy(which, side).start()

    def send_rows(which):
        source = fields[which]

        def pack(i, carry):
            row_send[which, 0, pl.ds(i, 1), :] = source[i, 0:1, :]
            row_send[which, 1, pl.ds(i, 1), :] = source[i, rows - 1 : rows, :]
            return carry

        lax.fori_loop(0, depth, pack, 0)
        for side in range(2):

            @pl.when(row_edges[side][0])
            def _():
                row_copy(which, side).start()

    def receive_rows(which):
        for side in range(2):

            @pl.when(row_edges[side][0])
            def _():
                row_copy(which, side).wait_send()
                row_copy(which, 1 - side).wait_recv()

    def receive_planes(which):
        for side in range(2):

            @pl.when(edges[side][0])
            def _():
                plane_copy(which, side).wait_send()
                plane_copy(which, 1 - side).wait_recv()

    send_planes(0)
    send_planes(1)
    loads[0].wait()
    send_rows(0)
    loads[1].wait()
    send_rows(1)

    half1 = 0.5 * dens[1]
    half_step = 0.5 * dens[0] - half1

    def half_density(value):
        return half1 + value * half_step

    edge_lane = lax.broadcasted_iota(jnp.int32, (SUB, LANES), 1)
    row = lax.broadcasted_iota(jnp.int32, (SUB, width), 0)
    first_row = row == 0
    last_row = row == SUB - 1
    tail = width - LANES

    def from_left(value, outside):
        turned = pltpu.roll(value, 1, 1)
        head = jnp.where(edge_lane == 0, outside, turned[:, :LANES])
        return jnp.concatenate([head, turned[:, LANES:]], axis=1)

    def from_right(value, outside):
        turned = pltpu.roll(value, width - 1, 1)
        end = jnp.where(edge_lane == LANES - 1, outside, turned[:, tail:])
        return jnp.concatenate([turned[:, :tail], end], axis=1)

    def here(block):
        return pl.ds(block * SUB, SUB)

    def wide(line):
        return jnp.broadcast_to(line, (SUB, width))

    def own_betas(i, before):
        turned_before = None
        for block in range(blocks):
            own = half_density(frac[i, here(block), :])
            beta2[i, here(block), :] = 1.0 / (own + from_left(own, half1))
            beta_last[i, here(block), :] = 1.0 / (own[:, tail:] + half1)
            if before:
                beta0[i, here(block), :] = 1.0 / (
                    own + half_density(frac[i - 1, here(block), :])
                )
            turned = pltpu.roll(own, 1, 0)
            south = turned
            if turned_before is not None:
                south = jnp.where(first_row, turned_before, turned)
            beta1[i, here(block), :] = 1.0 / (own + south)
            turned_before = turned

    def inner_betas(i, carry):
        own_betas(i, True)
        return carry

    own_betas(0, False)
    lax.fori_loop(1, depth, inner_betas, 0)

    receive_rows(0)
    for start in range(0, depth, SUB):
        part = pl.ds(start, SUB)
        low = half_density(row_send[0, 0, part, :]) + half_density(row_recv[0, 0, part, :])
        low = 1.0 / low
        for i in range(SUB):
            beta1[start + i, 0:1, :] = low[i : i + 1, :]
        high = half_density(row_send[0, 1, part, :]) + half_density(row_recv[0, 1, part, :])
        beta_top[part, :] = 1.0 / high

    def operator(which, i, before, after, emit):
        source = fields[which]
        turned_before = wide(row_recv[which, 0, pl.ds(i, 1), :])
        waiting = None
        for block in range(blocks):
            own = source[i, here(block), :]
            turned = pltpu.roll(own, 1, 0)
            south = jnp.where(first_row, turned_before, turned)
            flux1 = beta1[i, here(block), :] * (own - south)
            turned_flux = pltpu.roll(flux1, SUB - 1, 0)
            if waiting is not None:
                north = jnp.where(last_row, turned_flux, waiting[3])
                emit(waiting[0], waiting[1], waiting[2] - north)
            flux2 = beta2[i, here(block), :] * (own - from_left(own, 0.0))
            end = beta_last[i, here(block), :] * own[:, tail:]
            part = flux1 + (flux2 - from_right(flux2, -end))
            part = part + (
                beta0[i, here(block), :] * (own - before(block))
                + beta0[i + 1, here(block), :] * (own - after(block))
            )
            waiting = (block, own, part, turned_flux)
            turned_before = turned
        top = wide(beta_top[pl.ds(i, 1), :]) * (
            wide(row_recv[which, 1, pl.ds(i, 1), :]) - waiting[1]
        )
        north = jnp.where(last_row, top, waiting[3])
        emit(waiting[0], waiting[1], waiting[2] - north)

    def plane_of(which, i):
        source = fields[which]
        return lambda block: source[i, here(block), :]

    def halo_of(which, side):
        return lambda block: plane_recv[which, side, here(block), :]

    nothing = jnp.zeros((SUB, LANES), jnp.float32)

    def first_image(i, before, after, carry):
        sums = list(carry)

        def emit(block, own, result):
            image[i, here(block), :] = result
            sums[0] = sums[0] + fold(own * own)
            sums[1] = sums[1] + fold(own * result)

        operator(1, i, before, after, emit)
        return tuple(sums)

    def first_inner(i, carry):
        return first_image(i, plane_of(1, i - 1), plane_of(1, i + 1), carry)

    receive_rows(1)
    sums = lax.fori_loop(1, depth - 1, first_inner, (nothing, nothing))

    receive_planes(0)
    for block in range(blocks):
        low = half_density(frac[0, here(block), :])
        low = low + half_density(plane_recv[0, 0, here(block), :])
        beta0[0, here(block), :] = 1.0 / low
        high = half_density(frac[depth - 1, here(block), :])
        high = high + half_density(plane_recv[0, 1, here(block), :])
        beta0[depth, here(block), :] = 1.0 / high
    receive_planes(1)
    sums = first_image(0, halo_of(1, 0), plane_of(1, 1), sums)
    sums = first_image(depth - 1, plane_of(1, depth - 2), halo_of(1, 1), sums)

    unit = lax.broadcasted_iota(jnp.int32, (1, LANES), 1)

    def message(parts):
        value = jnp.zeros((1, LANES), jnp.float32)
        for place, part in enumerate(parts):
            value = jnp.where(unit == place, jnp.sum(part), value)
        return value

    def stage(phase, axis, buffer, send_sem, recv_sem, index, count):
        def copy(step):
            return pltpu.make_async_remote_copy(
                src_ref=buffer.at[phase, index],
                dst_ref=buffer.at[phase, index],
                send_sem=send_sem.at[phase, step],
                recv_sem=recv_sem.at[phase, step],
                device_id={axis: lax.rem(index + step, count)},
                device_id_type=MESH,
            )

        def start(value):
            buffer[phase, pl.ds(index, 1)] = value.reshape(1, 1, LANES)
            for step in range(1, count):
                copy(step).start()

        def finish():
            for step in range(1, count):
                copy(step).wait()
            total = buffer[phase, 0]
            for other in range(1, count):
                total = total + buffer[phase, other]
            return total

        return start, finish

    def across_grp(phase):
        return stage(phase, "grp", sum_grp, grp_send_sem, grp_recv_sem, g, groups)

    def across_dev(phase):
        return stage(phase, "dev", sum_dev, dev_send_sem, dev_recv_sem, d, devs)

    def pick(total, place):
        return jnp.sum(jnp.where(unit == place, total, 0.0), axis=1, keepdims=True)

    start_grp, finish_grp = across_grp(0)
    start_grp(message(sums))
    send_planes(2)
    send_rows(2)

    loads[2].wait()

    def advect(i, carry):
        for block in range(blocks):
            own = frac[i, here(block), :]
            speed = cour[i, here(block), :]
            head = jnp.where(edge_lane == 0, 0.0, speed[:, :LANES])
            speed = jnp.concatenate([head, speed[:, LANES:]], axis=1)
            left = from_left(own, 0.0)
            behind = own - left
            ahead = from_right(behind, -own[:, tail:])
            slope = jnp.maximum(0.0, jnp.minimum(ahead, behind)) + jnp.minimum(
                0.0, jnp.maximum(ahead, behind)
            )
            forward = speed > 0
            upwind = jnp.where(forward, left, own)
            tilt = jnp.where(forward, pltpu.roll(slope, 1, 1), -slope)
            flux = speed * (upwind + (0.5 - 0.5 * jnp.abs(speed)) * tilt)
            after = jnp.clip(own - (pltpu.roll(flux, width - 1, 1) - flux), 0.0, 1.0)
            flag = mask[pl.ds(block * SUB // TILE, 1), :]
            moved[i, here(block), :] = jnp.where(flag > 0.5, after, own)
        return carry

    half_way = depth // 2
    lax.fori_loop(0, half_way, advect, 0)
    start_dev, finish_dev = across_dev(0)
    start_dev(finish_grp())

    def second_image(i, before, after):
        def emit(block, own, result):
            second[i, here(block), :] = result

        operator(2, i, before, after, emit)

    def second_inner(i, carry):
        second_image(i, plane_of(2, i - 1), plane_of(2, i + 1))
        return carry

    receive_rows(2)
    lax.fori_loop(1, depth - 1, second_inner, 0)
    receive_planes(2)
    second_image(0, halo_of(2, 0), plane_of(2, 1))
    second_image(depth - 1, plane_of(2, depth - 2), halo_of(2, 1))

    total = finish_dev()
    norm0 = pick(total, 0)
    cross0 = pick(total, 1)
    alpha0 = norm0 / cross0

    def moments(i, carry):
        norm, mixed, cross = carry
        for block in range(blocks):
            ahead = image[i, here(block), :]
            left = field[i, here(block), :] - alpha0 * ahead
            norm = norm + fold(left * left)
            mixed = mixed + fold(left * ahead)
            cross = cross + fold(left * (ahead - alpha0 * second[i, here(block), :]))
        return norm, mixed, cross

    sums = lax.fori_loop(0, depth, moments, (nothing, nothing, nothing))
    start_grp, finish_grp = across_grp(1)
    start_grp(message(sums))
    three_quarters = half_way + (depth - half_way) // 2
    lax.fori_loop(half_way, three_quarters, advect, 0)
    start_dev, finish_dev = across_dev(1)
    start_dev(finish_grp())
    lax.fori_loop(three_quarters, depth, advect, 0)
    total = finish_dev()
    norm1 = pick(total, 0)
    mixed1 = pick(total, 1)
    cross1 = pick(total, 2)
    ratio = norm1 / norm0
    alpha1 = norm1 / (cross1 + ratio * (2.0 * mixed1 + ratio * cross0))
    factors[0:1, :] = jnp.broadcast_to(alpha0 + (alpha1 + alpha1 * ratio), (1, width))
    factors[1:2, :] = jnp.broadcast_to(alpha0 * alpha1, (1, width))


def closing(
    moved, field, image, second, factors, frac_out, pres_out, res_out, pres, res, sem
):
    depth, rows, width = moved.shape
    parts = 4
    size = depth // parts
    copies = [pltpu.make_async_copy(moved, frac_out, sem.at[0, parts])]
    copies[0].start()
    one = jnp.broadcast_to(factors[0:1, :], (SUB, width))
    two = jnp.broadcast_to(factors[1:2, :], (SUB, width))

    def finish(i, carry):
        for block in range(rows // SUB):
            here = pl.ds(block * SUB, SUB)
            begin = field[i, here, :]
            ahead = image[i, here, :]
            pres[i, here, :] = one * begin - two * ahead
            res[i, here, :] = begin - one * ahead + two * second[i, here, :]
        return carry

    for part in range(parts):
        lax.fori_loop(part * size, (part + 1) * size, finish, 0)
        planes = pl.ds(part * size, size)
        for place, (source, target) in enumerate(((pres, pres_out), (res, res_out))):
            copy = pltpu.make_async_copy(
                source.at[planes], target.at[planes], sem.at[place, part]
            )
            copy.start()
            copies.append(copy)
    for copy in copies:
        copy.wait()


def on_device(sizes, fraction, courant, divergence, densities, band_tiles):
    depth, rows, width = fraction.shape
    groups, devs = sizes
    block = (depth, rows, width)
    plain = pltpu.VMEM(block, jnp.float32)
    inside = pl.BlockSpec(memory_space=pltpu.VMEM)
    outside = pl.BlockSpec(memory_space=pltpu.HBM)
    held = pl.pallas_call(
        functools.partial(kernel, sizes),
        out_shape=(plain, plain, plain, plain, pltpu.VMEM((SUB, width), jnp.float32)),
        in_specs=[outside] * 3 + [pl.BlockSpec(memory_space=pltpu.SMEM)] * 2,
        out_specs=[inside] * 5,
        scratch_shapes=[
            plain,
            plain,
            pltpu.VMEM((depth + 1, rows, width), jnp.float32),
            plain,
            plain,
            pltpu.VMEM((depth, rows, LANES), jnp.float32),
            pltpu.VMEM((depth, width), jnp.float32),
            pltpu.VMEM((SUB, width), jnp.float32),
            pltpu.VMEM((3, 2, rows, width), jnp.float32),
            pltpu.VMEM((3, 2, depth, width), jnp.float32),
            pltpu.VMEM((3, 2, depth, width), jnp.float32),
            pltpu.VMEM((2, groups, 1, LANES), jnp.float32),
            pltpu.VMEM((2, devs, 1, LANES), jnp.float32),
            pltpu.SemaphoreType.DMA((3,)),
            pltpu.SemaphoreType.DMA((3, 2)),
            pltpu.SemaphoreType.DMA((3, 2)),
            pltpu.SemaphoreType.DMA((3, 2)),
            pltpu.SemaphoreType.DMA((3, 2)),
            pltpu.SemaphoreType.DMA((2, groups)),
            pltpu.SemaphoreType.DMA((2, groups)),
            pltpu.SemaphoreType.DMA((2, devs)),
            pltpu.SemaphoreType.DMA((2, devs)),
        ],
        compiler_params=pltpu.CompilerParams(
            collective_id=0, has_side_effects=True, vmem_limit_bytes=32 * MIB
        ),
        name="advance",
    )(fraction, courant, divergence, densities, band_tiles.reshape(-1))
    shape = jax.ShapeDtypeStruct(block, jnp.float32)
    return pl.pallas_call(
        closing,
        out_shape=(shape, shape, shape),
        in_specs=[inside] * 5,
        out_specs=[outside] * 3,
        scratch_shapes=[plain, plain, pltpu.SemaphoreType.DMA((2, 5))],
        compiler_params=pltpu.CompilerParams(vmem_limit_bytes=16 * MIB),
        name="closing",
    )(*held)


def solution(mesh):
    sizes = (mesh.shape["grp"], mesh.shape["dev"])
    placed = P("grp", "dev", None)
    return jax.shard_map(
        functools.partial(on_device, sizes),
        mesh=mesh,
        in_specs=(placed, placed, placed, P(), placed),
        out_specs=(placed, placed, placed),
        check_vma=False,
    )
```

time: 47.5 us -> 38.8 us (0.82)
  Pallas kernels: 39.7 us -> 31.9 us
  local copies, waits for them, and re-layouts: 6.98 us -> 6.07 us
    pallas_call x1 -> x2, Pallas kernels: 39.7 us -> 31.9 us  [the longest x1 29.1 us: on_device(): pl.pallas_call(functools.partial(kernel, sizes), out_shape=(plain, plain,...]
    unnamed x7 -> x10, local copies, waits for them, and re-layouts: 6.98 us -> 6.07 us
where the time goes in v2:
time: 38.8 us; the launch traced here: 38.6 us
  Pallas kernels  31.9 us (82%)
  local copies, waits for them, and re-layouts  6.07 us (16%)
  between operations  0.65 us (2%)
    pallas_call x1, Pallas kernels, on_device(): pl.pallas_call(functools.partial(kernel, sizes), out_shape=(plain, plain,...  29.1 us
    unnamed x10, local copies, waits for them, and re-layouts  6.07 us
    pallas_call x1, Pallas kernels, on_device(): pl.pallas_call(closing, out_shape=(shape, shape, shape), in_specs=[inside...  2.74 us

profile of v2, /device:TPU:0, one launch (start us, length us, event | category | flops | bytes accessed | tf_op | source)
XLA Modules:
  0.0 38.6 jit_solution(1025361550179866933)
XLA Ops:
  0.6 0.0 copy-start
  0.6 1.6 %copy-done = f32[16,32,1024]{2,1,0:T(8,128)S(1)} copy-done((f32[16,32,1024]{2,1,0:T(8,128)S(1)}, f32[16,32,1024]{2,1,0:T(8,128)}, u32[]{:S(2)}) %copy-start) | copy-done | bytes 2097176
  2.2 0.0 copy-start.1
  2.2 1.6 %copy-done.1 = f32[16,32,1024]{2,1,0:T(8,128)S(1)} copy-done((f32[16,32,1024]{2,1,0:T(8,128)S(1)}, f32[16,32,1024]{2,1,0:T(8,128)}, u32[]{:S(2)}) %copy-start.1) | copy-done | bytes 2097176
  3.8 0.0 copy-start.2
  3.8 1.6 %copy-done.2 = f32[16,32,1024]{2,1,0:T(8,128)S(1)} copy-done((f32[16,32,1024]{2,1,0:T(8,128)S(1)}, f32[16,32,1024]{2,1,0:T(8,128)}, u32[]{:S(2)}) %copy-start.2) | copy-done | bytes 2097176
  5.4 0.0 copy-start.3
  5.4 0.7 %copy-done.3 = f32[2]{0:T(128)S(1)} copy-done((f32[2]{0:T(128)S(1)}, f32[2]{0:T(128)}, u32[]{:S(2)}) %copy-start.3) | copy-done | bytes 32
  6.1 0.0 copy-start.4
  6.1 0.7 %copy-done.4 = s32[1,1,128]{2,1,0:T(1,128)S(1)} copy-done((s32[1,1,128]{2,1,0:T(1,128)S(1)}, s32[1,1,128]{2,1,0:T(1,128)}, u32[]{:S(2)}) %copy-start.4) | copy-done | bytes 536
  6.7 29.1 %advance.1 = (f32[16,32,1024]{2,1,0:T(8,128)S(1)}, f32[16,32,1024]{2,1,0:T(8,128)S(1)}, f32[16,32,1024]{2,1,0:T(8,128)S(1)}, f32[16,32,1024]{2,1,0:T(8,128)S(1)}, f32[8,1024]{1,0:T(8,128)S(1)}) custom-call(f32[16,32,1024]{2,1,0:T(8,128)S(1)} %copy-done, f32[16,32,1024]{2,1,0:T(8,128)S(1)} %copy-done.1, f32[16,32,1024]{2,1,0:T(8,128)S(1)} %copy-done.2, ...), custom_call_target="tpu_custom_call" | custom-call | tf_op jit(solution)/shard_map/advance/pallas_call | solution.py:477
  35.8 2.7 %closing.1 = (f32[16,32,1024]{2,1,0:T(8,128)}, f32[16,32,1024]{2,1,0:T(8,128)}, f32[16,32,1024]{2,1,0:T(8,128)}) custom-call(f32[16,32,1024]{2,1,0:T(8,128)S(1)} %get-tuple-element.8.moved, f32[16,32,1024]{2,1,0:T(8,128)S(1)} %get-tuple-element.9.field, f32[16,32,1024]{2,1,0:T(8,128)S(1)} %get-tuple-element.10.image, ...), custom_call_target="tpu_custom_call" | custom-call | tf_op jit(solution)/shard_map/closing/pallas_call | solution.py:512
Async XLA Ops:
  0.6 1.6 %copy-start = (f32[16,32,1024]{2,1,0:T(8,128)S(1)}, f32[16,32,1024]{2,1,0:T(8,128)}, u32[]{:S(2)}) copy-start(f32[16,32,1024]{2,1,0:T(8,128)} %frac_in.1) | copy-start | bytes 6291460
  2.2 1.6 %copy-start.1 = (f32[16,32,1024]{2,1,0:T(8,128)S(1)}, f32[16,32,1024]{2,1,0:T(8,128)}, u32[]{:S(2)}) copy-start(f32[16,32,1024]{2,1,0:T(8,128)} %cour_in.1) | copy-start | bytes 6291460
  3.8 1.6 %copy-start.2 = (f32[16,32,1024]{2,1,0:T(8,128)S(1)}, f32[16,32,1024]{2,1,0:T(8,128)}, u32[]{:S(2)}) copy-start(f32[16,32,1024]{2,1,0:T(8,128)} %div_in.1) | copy-start | bytes 6291460
  5.4 0.7 %copy-start.3 = (f32[2]{0:T(128)S(1)}, f32[2]{0:T(128)}, u32[]{:S(2)}) copy-start(f32[2]{0:T(128)} %dens.1) | copy-start | bytes 28
  6.1 0.7 %copy-start.4 = (s32[1,1,128]{2,1,0:T(1,128)S(1)}, s32[1,1,128]{2,1,0:T(1,128)}, u32[]{:S(2)}) copy-start(s32[1,1,128]{2,1,0:T(1,128)} %param.9) | copy-start | bytes 1540

commit v3 on v2

--- a/solution.py
+++ b/solution.py
@@ -474,6 +474,7 @@
     plain = pltpu.VMEM(block, jnp.float32)
     inside = pl.BlockSpec(memory_space=pltpu.VMEM)
     outside = pl.BlockSpec(memory_space=pltpu.HBM)
+    kept = [pltpu.with_memory_space_constraint(x, pltpu.HBM) for x in (fraction, courant, divergence)]
     held = pl.pallas_call(
         functools.partial(kernel, sizes),
         out_shape=(plain, plain, plain, plain, pltpu.VMEM((SUB, width), jnp.float32)),
@@ -504,10 +505,10 @@
             pltpu.SemaphoreType.DMA((2, devs)),
         ],
         compiler_params=pltpu.CompilerParams(
-            collective_id=0, has_side_effects=True, vmem_limit_bytes=32 * MIB
+            collective_id=0, has_side_effects=True, vmem_limit_bytes=55 * MIB
         ),
         name="advance",
-    )(fraction, courant, divergence, densities, band_tiles.reshape(-1))
+    )(*kept, densities, band_tiles.reshape(-1))
     shape = jax.ShapeDtypeStruct(block, jnp.float32)
     return pl.pallas_call(
         closing,

time: 38.8 us -> 32.4 us (0.84)
  local copies, waits for them, and re-layouts: 6.07 us -> 0 us
    unnamed x10 -> x0, local copies, waits for them, and re-layouts: 6.07 us -> none
where the time goes in v3:
time: 32.4 us; the launch traced here: 32.3 us
  Pallas kernels  31.6 us (98%)
  between operations  0.64 us (2%)
    pallas_call x1, Pallas kernels, on_device(): pl.pallas_call(functools.partial(kernel, sizes), out_shape=(plain, plain,...  28.9 us
    pallas_call x1, Pallas kernels, on_device(): pl.pallas_call(closing, out_shape=(shape, shape, shape), in_specs=[inside...  2.74 us

profile of v3, /device:TPU:0, one launch (start us, length us, event | category | flops | bytes accessed | tf_op | source)
XLA Modules:
  0.0 32.3 jit_solution(16313433904603610669)
XLA Ops:
  0.6 28.9 %advance.1 = (f32[16,32,1024]{2,1,0:T(8,128)S(1)}, f32[16,32,1024]{2,1,0:T(8,128)S(1)}, f32[16,32,1024]{2,1,0:T(8,128)S(1)}, f32[16,32,1024]{2,1,0:T(8,128)S(1)}, f32[8,1024]{1,0:T(8,128)S(1)}) custom-call(f32[16,32,1024]{2,1,0:T(8,128)} %frac_in.1, f32[16,32,1024]{2,1,0:T(8,128)} %cour_in.1, f32[16,32,1024]{2,1,0:T(8,128)} %div_in.1, f32[2]{0:T(128)} %dens.1, ...), custom_call_target="tpu_custom_call" | custom-call | tf_op jit(solution)/shard_map/advance/pallas_call | solution.py:478
  29.5 2.7 %closing.1 = (f32[16,32,1024]{2,1,0:T(8,128)}, f32[16,32,1024]{2,1,0:T(8,128)}, f32[16,32,1024]{2,1,0:T(8,128)}) custom-call(f32[16,32,1024]{2,1,0:T(8,128)S(1)} %get-tuple-element.8.moved, f32[16,32,1024]{2,1,0:T(8,128)S(1)} %get-tuple-element.9.field, f32[16,32,1024]{2,1,0:T(8,128)S(1)} %get-tuple-element.10.image, ...), custom_call_target="tpu_custom_call" | custom-call | tf_op jit(solution)/shard_map/closing/pallas_call | solution.py:513

commit v4 on v3

--- a/solution.py
+++ b/solution.py
@@ -44,17 +44,14 @@
     plane_recv,
     row_send,
     row_recv,
-    sum_grp,
-    sum_dev,
+    shared,
     load_sem,
     plane_send_sem,
     plane_recv_sem,
     row_send_sem,
     row_recv_sem,
-    grp_send_sem,
-    grp_recv_sem,
-    dev_send_sem,
-    dev_recv_sem,
+    sum_send_sem,
+    sum_recv_sem,
 ):
     groups, devs = sizes
     depth, rows, width = frac_in.shape
@@ -71,14 +68,15 @@
         loads.append(copy)
 
     barrier = pltpu.get_barrier_semaphore()
-    for step in range(1, groups):
-        pl.semaphore_signal(
-            barrier, inc=1, device_id={"grp": lax.rem(g + step, groups)}, device_id_type=MESH
-        )
-    for step in range(1, devs):
-        pl.semaphore_signal(
-            barrier, inc=1, device_id={"dev": lax.rem(d + step, devs)}, device_id_type=MESH
-        )
+    count = groups * devs
+    rank = g * devs + d
+
+    def partner(step):
+        other = lax.rem(rank + step, count)
+        return {"grp": other // devs, "dev": lax.rem(other, devs)}
+
+    for step in range(1, count):
+        pl.semaphore_signal(barrier, inc=1, device_id=partner(step), device_id_type=MESH)
 
     fields = (frac, field, image)
     edges = ((g > 0, g == 0), (g < groups - 1, g == groups - 1))
@@ -110,7 +108,7 @@
         0, across * along, listed, jnp.zeros((SUB, width), jnp.float32)
     )
 
-    pl.semaphore_wait(barrier, groups + devs - 2)
+    pl.semaphore_wait(barrier, count - 1)
 
     def plane_copy(which, side):
         plane = 0 if side == 0 else depth - 1
@@ -317,43 +315,34 @@
             value = jnp.where(unit == place, jnp.sum(part), value)
         return value
 
-    def stage(phase, axis, buffer, send_sem, recv_sem, index, count):
+    def all_devices(phase):
         def copy(step):
             return pltpu.make_async_remote_copy(
-                src_ref=buffer.at[phase, index],
-                dst_ref=buffer.at[phase, index],
-                send_sem=send_sem.at[phase, step],
-                recv_sem=recv_sem.at[phase, step],
-                device_id={axis: lax.rem(index + step, count)},
+                src_ref=shared.at[phase, rank],
+                dst_ref=shared.at[phase, rank],
+                send_sem=sum_send_sem.at[phase, step],
+                recv_sem=sum_recv_sem.at[phase, step],
+                device_id=partner(step),
                 device_id_type=MESH,
             )
 
         def start(value):
-            buffer[phase, pl.ds(index, 1)] = value.reshape(1, 1, LANES)
+            shared[phase, pl.ds(rank, 1)] = value.reshape(1, 1, LANES)
             for step in range(1, count):
                 copy(step).start()
 
         def finish():
             for step in range(1, count):
                 copy(step).wait()
-            total = buffer[phase, 0]
-            for other in range(1, count):
-                total = total + buffer[phase, other]
-            return total
+            return jnp.sum(shared[phase], axis=0)
 
         return start, finish
-
-    def across_grp(phase):
-        return stage(phase, "grp", sum_grp, grp_send_sem, grp_recv_sem, g, groups)
-
-    def across_dev(phase):
-        return stage(phase, "dev", sum_dev, dev_send_sem, dev_recv_sem, d, devs)
 
     def pick(total, place):
         return jnp.sum(jnp.where(unit == place, total, 0.0), axis=1, keepdims=True)
 
-    start_grp, finish_grp = across_grp(0)
-    start_grp(message(sums))
+    start_sums, finish_sums = all_devices(0)
+    start_sums(message(sums))
     send_planes(2)
     send_rows(2)
 
@@ -382,8 +371,6 @@
 
     half_way = depth // 2
     lax.fori_loop(0, half_way, advect, 0)
-    start_dev, finish_dev = across_dev(0)
-    start_dev(finish_grp())
 
     def second_image(i, before, after):
         def emit(block, own, result):
@@ -401,7 +388,7 @@
     second_image(0, halo_of(2, 0), plane_of(2, 1))
     second_image(depth - 1, plane_of(2, depth - 2), halo_of(2, 1))
 
-    total = finish_dev()
+    total = finish_sums()
     norm0 = pick(total, 0)
     cross0 = pick(total, 1)
     alpha0 = norm0 / cross0
@@ -417,14 +404,10 @@
         return norm, mixed, cross
 
     sums = lax.fori_loop(0, depth, moments, (nothing, nothing, nothing))
-    start_grp, finish_grp = across_grp(1)
-    start_grp(message(sums))
-    three_quarters = half_way + (depth - half_way) // 2
-    lax.fori_loop(half_way, three_quarters, advect, 0)
-    start_dev, finish_dev = across_dev(1)
-    start_dev(finish_grp())
-    lax.fori_loop(three_quarters, depth, advect, 0)
-    total = finish_dev()
+    start_sums, finish_sums = all_devices(1)
+    start_sums(message(sums))
+    lax.fori_loop(half_way, depth, advect, 0)
+    total = finish_sums()
     norm1 = pick(total, 0)
     mixed1 = pick(total, 1)
     cross1 = pick(total, 2)
@@ -492,17 +475,14 @@
             pltpu.VMEM((3, 2, rows, width), jnp.float32),
             pltpu.VMEM((3, 2, depth, width), jnp.float32),
             pltpu.VMEM((3, 2, depth, width), jnp.float32),
-            pltpu.VMEM((2, groups, 1, LANES), jnp.float32),
-            pltpu.VMEM((2, devs, 1, LANES), jnp.float32),
+            pltpu.VMEM((2, groups * devs, 1, LANES), jnp.float32),
             pltpu.SemaphoreType.DMA((3,)),
             pltpu.SemaphoreType.DMA((3, 2)),
             pltpu.SemaphoreType.DMA((3, 2)),
             pltpu.SemaphoreType.DMA((3, 2)),
             pltpu.SemaphoreType.DMA((3, 2)),
-            pltpu.SemaphoreType.DMA((2, groups)),
-            pltpu.SemaphoreType.DMA((2, groups)),
-            pltpu.SemaphoreType.DMA((2, devs)),
-            pltpu.SemaphoreType.DMA((2, devs)),
+            pltpu.SemaphoreType.DMA((2, groups * devs)),
+            pltpu.SemaphoreType.DMA((2, groups * devs)),
         ],
         compiler_params=pltpu.CompilerParams(
             collective_id=0, has_side_effects=True, vmem_limit_bytes=55 * MIB

time: 32.4 us -> 31.4 us (0.969)
  Pallas kernels: 31.6 us -> 30.6 us
    pallas_call x1, Pallas kernels: 28.9 us -> 27.9 us  [on_device(): pl.pallas_call(functools.partial(kernel, sizes), out_shape=(plain, plain,...]
where the time goes in v4:
time: 31.4 us; the launch traced here: 31.2 us
  Pallas kernels  30.6 us (97%)
  between operations  0.64 us (2%)
    pallas_call x1, Pallas kernels, on_device(): pl.pallas_call(functools.partial(kernel, sizes), out_shape=(plain, plain,...  27.9 us
    pallas_call x1, Pallas kernels, on_device(): pl.pallas_call(closing, out_shape=(shape, shape, shape), in_specs=[inside...  2.74 us

profile of v4, /device:TPU:0, one launch (start us, length us, event | category | flops | bytes accessed | tf_op | source)
XLA Modules:
  0.0 31.2 jit_solution(13970671042492997804)
XLA Ops:
  0.6 27.9 %advance.1 = (f32[16,32,1024]{2,1,0:T(8,128)S(1)}, f32[16,32,1024]{2,1,0:T(8,128)S(1)}, f32[16,32,1024]{2,1,0:T(8,128)S(1)}, f32[16,32,1024]{2,1,0:T(8,128)S(1)}, f32[8,1024]{1,0:T(8,128)S(1)}) custom-call(f32[16,32,1024]{2,1,0:T(8,128)} %frac_in.1, f32[16,32,1024]{2,1,0:T(8,128)} %cour_in.1, f32[16,32,1024]{2,1,0:T(8,128)} %div_in.1, f32[2]{0:T(128)} %dens.1, ...), custom_call_target="tpu_custom_call" | custom-call | tf_op jit(solution)/shard_map/advance/pallas_call | solution.py:461
  28.5 2.7 %closing.1 = (f32[16,32,1024]{2,1,0:T(8,128)}, f32[16,32,1024]{2,1,0:T(8,128)}, f32[16,32,1024]{2,1,0:T(8,128)}) custom-call(f32[16,32,1024]{2,1,0:T(8,128)S(1)} %get-tuple-element.8.moved, f32[16,32,1024]{2,1,0:T(8,128)S(1)} %get-tuple-element.9.field, f32[16,32,1024]{2,1,0:T(8,128)S(1)} %get-tuple-element.10.image, ...), custom_call_target="tpu_custom_call" | custom-call | tf_op jit(solution)/shard_map/closing/pallas_call | solution.py:493
